TPU v7x, 32 devices: a whole 2x2x4 slice. The times are simulated.
32 devices in a mesh: dp: 16 (over z, y, x), mp: 2 (over core).
Axes of the slice: x: 2, y: 2, z: 4, core: 2. Of those that a mesh axis runs over, the one named last changes fastest.
Arguments:
- clean: float32 [64, 3, 4096], P(('dp', 'mp')), may hold values from -1 to 1
- noise: float32 [64, 3, 4096], P(('dp', 'mp')), may hold values from -12 to 12
- lowres: float32 [64, 3, 4096], P(('dp', 'mp')), may hold values from -1 to 1
- aug_noise: float32 [64, 3, 4096], P(('dp', 'mp')), may hold values from -5 to 5
- timesteps: int32 [64], P(('dp', 'mp')), may hold values from 0 to 999
- aug_levels: int32 [64], P(('dp', 'mp')), may hold values from 0 to 999
- lengths: int32 [64], P(('dp', 'mp')), may hold values from 1 to 128
- text: bfloat16 [64, 128, 4096], P(('dp', 'mp')), may hold values from -160 to 160
- w_stem: float32 [6, 128], replicated, may hold values from -2.5 to 2.5
- w_time: float32 [256, 256], replicated, may hold values from -0.375 to 0.375
- conv_one: bfloat16 [1152, 128], replicated, may hold values from -0.1875 to 0.1875
- conv_two: bfloat16 [1152, 128], replicated, may hold values from -0.1875 to 0.1875
- kv_weight: bfloat16 [4096, 256], P('mp'), may hold values from -0.09375 to 0.09375
- w_query: bfloat16 [128, 128], replicated, may hold values from -0.5 to 0.5
- w_output: bfloat16 [128, 128], replicated, may hold values from -0.5 to 0.5
- w_head: bfloat16 [3, 128], replicated, may hold values from -0.5 to 0.5
Outputs:
- conv_one_update: float32 [1152, 128], P(('dp', 'mp'))
- conv_two_update: float32 [1152, 128], P(('dp', 'mp'))
- kv_update: float32 [4096, 256], P('mp', 'dp')
- loss_mean: float32 [], replicated
All inputs are finite; a program needn't handle non-finite values.
Results may differ from a plain program's by a relative error of at most 0.03.
The roundings to bfloat16 on the way count: a program that leaves them out, or rounds other values in their place, can miss the bound.
Values may be sent and summed in bfloat16 or wider, within the bound.
A program may use at most 128 MiB of HBM per device.

v0:
```python
import math

import jax
import jax.numpy as jnp
from jax import lax
from jax.sharding import PartitionSpec as P

S = 64
GROUPS = 32
HEADS = 2
HEAD_DIM = 64
FREQS = 64
STEPS = 1000


def signal_level(index):
    ratio = (index.astype(jnp.float32) / STEPS + 0.008) / 1.008
    cosine = jnp.cos(ratio * (math.pi / 2.0))
    return cosine * cosine


def sinusoid(index):
    freqs = jnp.exp(-math.log(10000.0) * jnp.arange(FREQS, dtype=jnp.float32) / FREQS)
    angles = index.astype(jnp.float32) * freqs
    return jnp.concatenate([jnp.sin(angles), jnp.cos(angles)])


def prepare(clean, noise, lowres, aug_noise, tstep, level, w_stem, w_time):
    signal = signal_level(tstep)
    aug_signal = signal_level(level)
    noisy = jnp.sqrt(signal) * clean + jnp.sqrt(1.0 - signal) * noise
    low_noisy = jnp.sqrt(aug_signal) * lowres + jnp.sqrt(1.0 - aug_signal) * aug_noise
    stacked = jnp.concatenate([noisy, low_noisy], axis=0)
    h_start = jnp.einsum("kp,kc->pc", stacked, w_stem, precision=lax.Precision.HIGHEST)
    feature = jnp.concatenate([sinusoid(tstep), sinusoid(level)])[None, :]
    embed = jax.nn.silu(jnp.dot(feature, w_time, precision=lax.Precision.HIGHEST))[0]
    channels = w_stem.shape[1]
    return (h_start, embed[:channels], embed[channels:])


def group_matrix(channels):
    members = channels // GROUPS
    labels = jnp.arange(channels) // members
    return (labels[:, None] == labels[None, :]).astype(jnp.float32) / members


def group_norm(values, grouping):
    average = jnp.dot(
        jnp.mean(values, axis=0, keepdims=True), grouping, precision=lax.Precision.HIGHEST
    )
    centred = values - average
    spread = jnp.dot(
        jnp.mean(centred * centred, axis=0, keepdims=True),
        grouping,
        precision=lax.Precision.HIGHEST,
    )
    return centred * lax.rsqrt(spread + 1e-05)


def convolve(activation, weight):
    channels = weight.shape[1]
    kernel = weight.reshape(3, 3, channels, channels)
    picture = activation.reshape(1, S, S, channels)
    result = lax.conv_general_dilated(
        picture,
        kernel,
        (1, 1),
        "SAME",
        dimension_numbers=("NHWC", "HWIO", "NHWC"),
        preferred_element_type=jnp.float32,
    )
    return result.reshape(S * S, channels)


def image_loss(
    conv_one, conv_two, keys_values, h_start, scale, shift, keep, w_query, w_output, w_head, noise
):
    channels = conv_one.shape[1]
    grouping = group_matrix(channels)
    act_one = jax.nn.silu(group_norm(h_start, grouping)).astype(jnp.bfloat16)
    conv_out_one = convolve(act_one, conv_one)
    act_two = jax.nn.silu(group_norm(conv_out_one, grouping) * (1.0 + scale) + shift).astype(
        jnp.bfloat16
    )
    h_mid = h_start + convolve(act_two, conv_two)
    normed = group_norm(h_mid, grouping).astype(jnp.bfloat16)
    queries = (
        jnp.dot(normed, w_query, preferred_element_type=jnp.float32) * HEAD_DIM ** (-0.5)
    ).astype(jnp.bfloat16)
    width = w_query.shape[1]
    pieces = []
    for head_index in range(HEADS):
        lower = head_index * HEAD_DIM
        upper = lower + HEAD_DIM
        scores = jnp.dot(
            queries[:, lower:upper],
            keys_values[:, lower:upper].T,
            preferred_element_type=jnp.float32,
        )
        scores = jnp.where(keep[None, :], scores, -1e30)
        highest = jnp.max(scores, axis=1, keepdims=True)
        weights = jnp.exp(scores - highest)
        probs = (weights / jnp.sum(weights, axis=1, keepdims=True)).astype(jnp.bfloat16)
        pieces.append(
            jnp.dot(
                probs,
                keys_values[:, width + lower : width + upper],
                preferred_element_type=jnp.float32,
            )
        )
    attended = jnp.concatenate(pieces, axis=1).astype(jnp.bfloat16)
    h_out = h_mid + jnp.dot(attended, w_output, preferred_element_type=jnp.float32)
    pred = jnp.einsum(
        "kc,pc->kp", w_head, h_out.astype(jnp.bfloat16), preferred_element_type=jnp.float32
    )
    error = pred - noise
    return jnp.sum(error * error)


def local(
    clean,
    noise,
    lowres,
    aug_noise,
    timesteps,
    aug_levels,
    lengths,
    text,
    w_stem,
    w_time,
    conv_one,
    conv_two,
    kv_weight,
    w_query,
    w_output,
    w_head,
):
    images = clean.shape[0]
    tokens = text.shape[1]
    features = text.shape[2]
    width = kv_weight.shape[1]
    half = kv_weight.shape[0]
    piece = lax.all_gather(kv_weight, "mp", axis=0, tiled=True)
    flat = jnp.dot(
        text.reshape(images * tokens, piece.shape[0]), piece, preferred_element_type=jnp.float32
    )
    summed = flat.reshape(images, tokens, width)
    keys_values = summed.astype(jnp.bfloat16)

    def one_image(items):
        clean_i, noise_i, low_i, aug_i, tstep, level, length, pairs = items
        h_start, scale, shift = prepare(
            clean_i, noise_i, low_i, aug_i, tstep, level, w_stem, w_time
        )
        keep = jnp.arange(tokens) < length
        value, pullback = jax.vjp(
            lambda first, second, third: image_loss(
                first,
                second,
                third,
                h_start,
                scale,
                shift,
                keep,
                w_query,
                w_output,
                w_head,
                noise_i,
            ),
            conv_one,
            conv_two,
            pairs,
        )
        part_one, part_two, part_kv = pullback(jnp.ones((), jnp.float32))
        return (part_one, part_two, part_kv, value)

    parts_one, parts_two, parts_kv, values = lax.map(
        one_image, (clean, noise, lowres, aug_noise, timesteps, aug_levels, lengths, keys_values)
    )
    local_one = jnp.sum(parts_one.astype(jnp.float32), axis=0)
    local_two = jnp.sum(parts_two.astype(jnp.float32), axis=0)
    local_loss = jnp.sum(values)
    loss_total = lax.psum(local_loss, ("dp", "mp"))
    grad_one, grad_two = (
        lax.psum_scatter(local_one, ("dp", "mp"), scatter_dimension=0, tiled=True),
        lax.psum_scatter(local_two, ("dp", "mp"), scatter_dimension=0, tiled=True),
    )
    full_grad = lax.dot_general(
        text.reshape(-1, features),
        parts_kv.reshape(-1, width),
        (((0,), (0,)), ((), ())),
        preferred_element_type=jnp.float32,
    )
    row_share = lax.psum_scatter(full_grad, "mp", scatter_dimension=0, tiled=True)
    grad_kv = lax.psum_scatter(row_share, "dp", scatter_dimension=1, tiled=True)
    square_one = jnp.sum(grad_one * grad_one)
    square_two = jnp.sum(grad_two * grad_two)
    square_kv = jnp.sum(grad_kv * grad_kv)
    total_one, total_two, total_kv = lax.psum((square_one, square_two, square_kv), ("dp", "mp"))
    conv_count = conv_one.shape[0] * conv_one.shape[1]
    kv_count = half * lax.axis_size("mp") * width
    conv_one_update = grad_one * lax.rsqrt(total_one / conv_count + 1e-06)
    conv_two_update = grad_two * lax.rsqrt(total_two / conv_count + 1e-06)
    kv_update = grad_kv * lax.rsqrt(total_kv / kv_count + 1e-06)
    loss_mean = loss_total / (
        images * lax.axis_size(("dp", "mp")) * clean.shape[1] * clean.shape[2]
    )
    return (conv_one_update, conv_two_update, kv_update, loss_mean)


def solution(mesh):
    return jax.shard_map(
        local,
        mesh=mesh,
        in_specs=(
            P(("dp", "mp"), None, None),
            P(("dp", "mp"), None, None),
            P(("dp", "mp"), None, None),
            P(("dp", "mp"), None, None),
            P(("dp", "mp")),
            P(("dp", "mp")),
            P(("dp", "mp")),
            P(("dp", "mp"), None, None),
            P(),
            P(),
            P(),
            P(),
            P("mp", None),
            P(),
            P(),
            P(),
        ),
        out_specs=(P(("dp", "mp"), None), P(("dp", "mp"), None), P("mp", "dp"), P()),
        check_vma=False,
    )
```

profile of v0, /device:TPU:0, one launch (start us, length us, event | category | flops | bytes accessed | tf_op | source)
XLA Modules:
  0.0 415.6 jit_solution(3835564456848357906)
XLA Ops:
  8.1 14.8 %all-gather.2.cloned.1.call-done = bf16[4096,256]{1,0:T(8,128)(2,1)} async-done(((bf16[2048,256]{1,0:T(8,128)(2,1)}), bf16[4096,256]{1,0:T(8,128)(2,1)}) %all-gather.2.cloned.1.call-update) | async-done | bytes 2097168 | tf_op jit(solution)/shard_map/all_gather | solution.py:143
  22.9 2.9 fusion.285
  25.8 184.8 %while.19 = (s32[]{:T(128)}, bf16[2,1152,128]{2,1,0:T(8,128)(2,1)}, bf16[2,1152,128]{2,1,0:T(8,128)(2,1)}, bf16[2,128,256]{1,2,0:T(8,128)(2,1)}, f32[2]{0:T(128)...) while((s32[]{:T(128)}, bf16[2,1152,128]{2,1,0:T(8,128)(2,1)}, ...), condition=%wide.region_22.23_spmd, body=%wide.region_0.22_spmd.sunk | while | flops 8245876736 | bytes 325935616 | solution.py:177
  33.1 3.5 fusion.464
  40.1 3.0 select_reduce_fusion.8
  46.1 1.2 fusion.474
  48.2 3.1 fusion.476
  51.9 1.2 copy.133
  58.1 2.1 convert_reduce_fusion.7
  60.2 1.1 convolution_convert_fusion.20
  62.2 2.1 convert_reduce_fusion.6
  65.4 1.2 convolution_convert_fusion.19
  66.6 3.9 multiply_reduce_fusion.17
  70.5 1.5 convolution_convert_fusion.21
  72.0 1.4 convolution_convert_fusion.22
  82.2 1.5 multiply_reduce_fusion.20
  88.3 5.1 %select_reduce_fusion.10 = (f32[128]{0:T(128)S(1)}, f32[64,8,9,128]{3,1,2,0:T(8,128)S(1)}) fusion(f32[64,8,9,128]{3,1,2,0:T(8,128)S(1)} %copy-done.8, f32[128]{0:T(128)S(1)} %copy-done.40, pred[8,9]{0,1:T(8,128)(4,1)} %get-tuple-element.839, f32[128]{0:T(128)S(1)} %copy-done.48, f32[128]{0:T(128)S(1)} %copy-done.46, f32[128]{0:T(128)S(1)} %copy-done.50, ...), kind=kOutput, calls=%fused_computation.51.clone.1 | convolution fusion | flops 1360920448 | bytes 6425160 | tf_op jit(solution)/shard_map/while/body/eval_jaxpr/transpose(jvp())/conv_general_dilated | solution.py:64
  93.6 1.4 select_reduce_fusion.11
  98.4 5.0 %fusion.499 = bf16[3,3,128,128,1]{3,2,1,4,0:T(8,128)(2,1)S(1)} fusion(bf16[64,8,9,128,1]{3,1,4,2,0:T(8,128)(2,1)S(1)} %fusion.495, bf16[64,8,9,128,1]{3,1,4,2,0:T(8,128)(2,1)S(1)} %copy.137, bf16[64,8,9,128,1]{3,1,4,2,0:T(8,128)(2,1)S(1)} %fusion.496, f32[128]{0:T(128)S(1)} %fusion.498, pred[8,9]{0,1:T(8,128)(4,1)} %get-tuple-element.839, ...), kind=kOutput, calls=%fused_computation.101.clone.1 | convolution fusion | flops 1360281600 | bytes 8554568 | tf_op jit(solution)/shard_map/while/body/eval_jaxpr/transpose(jvp())/conv_general_dilated | solution.py:64
  103.4 1.8 fusion.491
  106.5 4.8 %fusion.492 = bf16[3,3,128,128,1]{3,2,1,4,0:T(8,128)(2,1)S(1)} fusion(bf16[64,8,9,128,1]{3,0,2,1,4:T(8,128)(2,1)S(1)} %bitcast.331, bf16[64,8,9,128,1]{3,1,2,0,4:T(8,128)(2,1)S(1)} %maximum_bitcast_fusion.8, bf16[64,8,9,128,1]{3,1,2,0,4:T(8,128)(2,1)S(1)} %fusion.491, bf16[64,8,9,128,1]{3,1,2,0,4:T(8,128)(2,1)S(1)} %maximum_bitcast_fusion.9), kind=kOutput, calls=%fused_computation.100.clone.1 | convolution fusion | flops 1348337664 | bytes 5013504 | tf_op jit(solution)/shard_map/while/body/eval_jaxpr/transpose(jvp())/conv_general_dilated | solution.py:64
  123.4 3.5 fusion.464
  130.5 3.0 select_reduce_fusion.8
  136.4 1.4 fusion.474
  138.7 3.1 fusion.476
  142.5 1.2 copy.133
  148.6 2.1 convert_reduce_fusion.7
  152.8 2.1 convert_reduce_fusion.6
  155.9 1.2 convolution_convert_fusion.19
  157.2 3.9 multiply_reduce_fusion.17
  161.1 1.5 convolution_convert_fusion.21
  162.6 1.4 convolution_convert_fusion.22
  172.8 1.5 multiply_reduce_fusion.20
  178.9 4.9 %select_reduce_fusion.10 = (f32[128]{0:T(128)S(1)}, f32[64,8,9,128]{3,1,2,0:T(8,128)S(1)}) fusion(f32[64,8,9,128]{3,1,2,0:T(8,128)S(1)} %copy-done.8, f32[128]{0:T(128)S(1)} %copy-done.40, pred[8,9]{0,1:T(8,128)(4,1)} %get-tuple-element.839, f32[128]{0:T(128)S(1)} %copy-done.48, f32[128]{0:T(128)S(1)} %copy-done.46, f32[128]{0:T(128)S(1)} %copy-done.50, ...), kind=kOutput, calls=%fused_computation.51.clone.1 | convolution fusion | flops 1360920448 | bytes 6425160 | tf_op jit(solution)/shard_map/while/body/eval_jaxpr/transpose(jvp())/conv_general_dilated | solution.py:64
  184.0 1.4 select_reduce_fusion.11
  188.8 5.0 %fusion.499 = bf16[3,3,128,128,1]{3,2,1,4,0:T(8,128)(2,1)S(1)} fusion(bf16[64,8,9,128,1]{3,1,4,2,0:T(8,128)(2,1)S(1)} %fusion.495, bf16[64,8,9,128,1]{3,1,4,2,0:T(8,128)(2,1)S(1)} %copy.137, bf16[64,8,9,128,1]{3,1,4,2,0:T(8,128)(2,1)S(1)} %fusion.496, f32[128]{0:T(128)S(1)} %fusion.498, pred[8,9]{0,1:T(8,128)(4,1)} %get-tuple-element.839, ...), kind=kOutput, calls=%fused_computation.101.clone.1 | convolution fusion | flops 1360281600 | bytes 8554568 | tf_op jit(solution)/shard_map/while/body/eval_jaxpr/transpose(jvp())/conv_general_dilated | solution.py:64
  193.8 1.8 fusion.491
  196.8 5.0 %fusion.492 = bf16[3,3,128,128,1]{3,2,1,4,0:T(8,128)(2,1)S(1)} fusion(bf16[64,8,9,128,1]{3,0,2,1,4:T(8,128)(2,1)S(1)} %bitcast.331, bf16[64,8,9,128,1]{3,1,2,0,4:T(8,128)(2,1)S(1)} %maximum_bitcast_fusion.8, bf16[64,8,9,128,1]{3,1,2,0,4:T(8,128)(2,1)S(1)} %fusion.491, bf16[64,8,9,128,1]{3,1,2,0,4:T(8,128)(2,1)S(1)} %maximum_bitcast_fusion.9), kind=kOutput, calls=%fused_computation.100.clone.1 | convolution fusion | flops 1348337664 | bytes 5013504 | tf_op jit(solution)/shard_map/while/body/eval_jaxpr/transpose(jvp())/conv_general_dilated | solution.py:64
  210.7 3.6 convolution_bitcast_fusion.11
  214.4 13.2 %reduce-scatter.7.cloned.1.call-done = f32[2048,256]{0,1:T(8,128)} async-done(((f32[4096,256]{0,1:T(8,128)}), f32[2048,256]{0,1:T(8,128)}) %reduce-scatter.7.cloned.1.call-update) | async-done | bytes 2097168 | tf_op jit(solution)/shard_map/reduce_scatter | solution.py:194
  227.6 1.5 convert_reduce_fusion.2
  229.2 86.5 %fusion.288 = (f32[48,128]{1,0:T(8,128)S(1)}, f32[48,128]{1,0:T(8,128)S(1)}) fusion(f32[1152,128]{1,0:T(8,128)S(1)} %get-tuple-element.470, f32[1152,128]{1,0:T(8,128)S(1)} %get-tuple-element.469), kind=kCustom, calls=%all-reduce-scatter.2 | all-reduce-scatter fusion | flops 393217 | bytes 1228800
  315.7 1.3 collective-permute-start.15
  317.0 1.3 collective-permute-start.10
  318.3 1.3 collective-permute-start.11
  319.6 1.3 collective-permute-start.12
  320.9 1.3 collective-permute-start.13
  322.2 7.0 %collective-permute-start.7 = (f32[36,128]{1,0:T(8,128)S(1)}, f32[36,128]{1,0:T(8,128)S(1)}, u32[]{:S(2)}, u32[]{:S(2)}) collective-permute-start(f32[36,128]{1,0:T(8,128)S(1)} %slice.90), channel_id=1, source_target_pairs={{0,8},{1,9},{2,10},{3,11},{4,12},{5,13},{6,14},{7,15},{8,16},{9,17... | collective-permute-start | bytes 55304
  329.2 1.5 collective-permute-done.7
  330.7 1.3 collective-permute-start.14
  332.0 4.9 %collective-permute-start.8 = (f32[48,128]{1,0:T(8,128)S(1)}, f32[48,128]{1,0:T(8,128)S(1)}, u32[]{:S(2)}, u32[]{:S(2)}) collective-permute-start(f32[48,128]{1,0:T(8,128)S(1)} %get-tuple-element.418), channel_id=1, source_target_pairs={{0,1},{1,2},{2,3},{3,4},{4,5},{5,6},{6,7},{7,8},{8,9},{9,10},{10,1... | collective-permute-start | bytes 73736
  336.9 2.8 collective-permute-start.9
  339.7 2.6 collective-permute-start
  342.3 3.2 collective-permute-start.1
  345.5 2.9 collective-permute-start.2
  348.5 2.4 collective-permute-start.3
  350.9 2.0 collective-permute-start.4
  352.9 3.0 collective-permute-start.5
  355.9 1.6 collective-permute-start.6
  358.2 1.2 concatenate.34
  359.4 1.2 concatenate.33
  361.9 1.5 multiply_reduce_fusion.6
  363.5 38.8 %all-reduce.10 = (f32[]{:T(128)}, f32[]{:T(128)}, f32[]{:T(128)}, f32[]{:T(128)}) all-reduce(f32[]{:T(128)} %multiply_reduce_fusion.8, f32[]{:T(128)} %multiply_reduce_fusion.7, f32[]{:T(128)} %multiply_reduce_fusion.6, f32[]{:T(128)} %reduce_sum.338), channel_id=1, replica_groups=mesh['dp'=16,'mp'=2] {'dp','mp'}, use_global_device_ids=true, to_apply=%region_26.27 | all-reduce | flops 4 | bytes 32 | tf_op jit(solution)/shard_map/psum | solution.py:199
  406.2 1.6 broadcast_multiply_fusion
  (474 shorter events, 82.6 us)
Async XLA Ops:
  7.2 15.7 %copy-start = (bf16[2,128,4096]{2,1,0:T(8,128)(2,1)S(1)}, bf16[2,128,4096]{2,1,0:T(8,128)(2,1)}, u32[]{:S(2)}) copy-start(bf16[2,128,4096]{2,1,0:T(8,128)(2,1)} %param.25) | copy-start | bytes 6291460
  7.2 15.7 %all-gather.2.cloned.1.call-start = ((), (), s32[]{:S(2)}) async-start(), calls=%async_computation.2 | async-start | bytes 3145728 | tf_op jit(solution)/shard_map/all_gather | solution.py:143
  7.9 219.7 %reduce-scatter.7.cloned.1.call-start = ((), (), s32[]{:S(2)}) async-start(), calls=%async_computation.3 | async-start | bytes 6291456 | tf_op jit(solution)/shard_map/reduce_scatter | solution.py:194
  8.0 17.8 %copy-start.26 = (bf16[128,128]{1,0:T(8,128)(2,1)S(1)}, bf16[128,128]{1,0:T(8,128)(2,1)}, u32[]{:S(2)}) copy-start(bf16[128,128]{1,0:T(8,128)(2,1)} %param.31) | copy-start | bytes 98308
  8.0 17.8 %copy-start.30 = (pred[8,9]{0,1:T(8,128)(4,1)S(1)}, pred[8,9]{0,1:T(8,128)(4,1)}, u32[]{:S(2)}) copy-start(pred[8,9]{0,1:T(8,128)(4,1)} %constant.595) | copy-start | bytes 220
  8.0 17.8 %copy-start.53 = (f32[6,128]{1,0:T(8,128)S(1)}, f32[6,128]{1,0:T(8,128)}, u32[]{:S(2)}) copy-start(f32[6,128]{1,0:T(8,128)} %param.26) | copy-start | bytes 9220
  8.0 17.8 %copy-start.58 = (s32[2]{0:T(128)S(1)}, s32[2]{0:T(128)}, u32[]{:S(2)}) copy-start(s32[2]{0:T(128)} %param.22) | copy-start | bytes 28
  8.0 17.8 %copy-start.60 = (s32[2]{0:T(128)S(1)}, s32[2]{0:T(128)}, u32[]{:S(2)}) copy-start(s32[2]{0:T(128)} %param.23) | copy-start | bytes 28
  8.1 17.8 %copy-start.62 = (s32[2]{0:T(128)S(1)}, s32[2]{0:T(128)}, u32[]{:S(2)}) copy-start(s32[2]{0:T(128)} %param.24) | copy-start | bytes 28
  36.5 18.0 %copy-start.67 = (s32[128]{0:T(128)}, s32[128]{0:T(128)S(1)}, u32[]{:S(2)}) copy-start(s32[128]{0:T(128)S(1)} %and_select_fusion.2) | copy-start | bytes 1540 | tf_op jit(solution)/shard_map/while
  43.2 4.1 copy-start.7
  47.3 4.0 copy-start.9
  55.9 5.5 %copy-start.15 = (bf16[4096,128]{0,1:T(8,128)(2,1)}, bf16[4096,128]{0,1:T(8,128)(2,1)S(1)}, u32[]{:S(2)}) copy-start(bf16[4096,128]{0,1:T(8,128)(2,1)S(1)} %fusion.479) | copy-start | bytes 3145732 | tf_op jit(solution)/shard_map/while
  57.3 4.1 copy-start.41
  58.1 3.3 copy-start.21
  62.2 4.4 %copy-start.23 = (f32[4096]{0:T(1024)}, f32[4096]{0:T(1024)S(1)}, u32[]{:S(2)}) copy-start(f32[4096]{0:T(1024)S(1)} %fusion.481) | copy-start | bytes 49156 | tf_op jit(solution)/shard_map/while
  70.5 3.0 copy-start.24
  70.5 3.0 copy-start.6
  88.3 5.1 %copy-start.69 = (f32[128]{0:T(128)S(1)}, f32[128]{0:T(128)}, u32[]{:S(2)}) copy-start(f32[128]{0:T(128)} %get-tuple-element.687) | copy-start | bytes 1540 | tf_op jit(solution)/shard_map/while
  106.3 4.9 %copy-start.33 = (bf16[2,1152,128]{2,1,0:T(8,128)(2,1)S(1)}, bf16[2,1152,128]{2,1,0:T(8,128)(2,1)}, u32[]{:S(2)}) copy-start(bf16[2,1152,128]{2,1,0:T(8,128)(2,1)} %get-tuple-element.720) | copy-start | bytes 1769476 | tf_op jit(solution)/shard_map/while
  106.4 4.9 %copy-start.35 = (bf16[2,1152,128]{2,1,0:T(8,128)(2,1)S(1)}, bf16[2,1152,128]{2,1,0:T(8,128)(2,1)}, u32[]{:S(2)}) copy-start(bf16[2,1152,128]{2,1,0:T(8,128)(2,1)} %get-tuple-element.721) | copy-start | bytes 1769476 | tf_op jit(solution)/shard_map/while
  106.4 5.0 %copy-start.64 = (f32[2]{0:T(128)S(1)}, f32[2]{0:T(128)}, u32[]{:S(2)}) copy-start(f32[2]{0:T(128)} %get-tuple-element.723) | copy-start | bytes 28 | tf_op jit(solution)/shard_map/while
  106.4 6.3 %copy-start.27 = (bf16[128,128]{1,0:T(8,128)(2,1)S(1)}, bf16[128,128]{1,0:T(8,128)(2,1)}, u32[]{:S(2)}) copy-start(bf16[128,128]{1,0:T(8,128)(2,1)} %get-tuple-element.805) | copy-start | bytes 98308 | tf_op jit(solution)/shard_map/while
  106.4 6.3 %copy-start.31 = (pred[8,9]{0,1:T(8,128)(4,1)S(1)}, pred[8,9]{0,1:T(8,128)(4,1)}, u32[]{:S(2)}) copy-start(pred[8,9]{0,1:T(8,128)(4,1)} %get-tuple-element.839) | copy-start | bytes 220 | tf_op jit(solution)/shard_map/while
  106.4 6.2 %copy-start.54 = (f32[6,128]{1,0:T(8,128)S(1)}, f32[6,128]{1,0:T(8,128)}, u32[]{:S(2)}) copy-start(f32[6,128]{1,0:T(8,128)} %get-tuple-element.884) | copy-start | bytes 9220 | tf_op jit(solution)/shard_map/while
  106.4 6.2 %copy-start.59 = (s32[2]{0:T(128)S(1)}, s32[2]{0:T(128)}, u32[]{:S(2)}) copy-start(s32[2]{0:T(128)} %get-tuple-element.934) | copy-start | bytes 28 | tf_op jit(solution)/shard_map/while
  106.4 6.2 %copy-start.61 = (s32[2]{0:T(128)S(1)}, s32[2]{0:T(128)}, u32[]{:S(2)}) copy-start(s32[2]{0:T(128)} %get-tuple-element.966) | copy-start | bytes 28 | tf_op jit(solution)/shard_map/while
  106.4 6.2 %copy-start.63 = (s32[2]{0:T(128)S(1)}, s32[2]{0:T(128)}, u32[]{:S(2)}) copy-start(s32[2]{0:T(128)} %get-tuple-element.999) | copy-start | bytes 28 | tf_op jit(solution)/shard_map/while
  126.9 18.2 %copy-start.67 = (s32[128]{0:T(128)}, s32[128]{0:T(128)S(1)}, u32[]{:S(2)}) copy-start(s32[128]{0:T(128)S(1)} %and_select_fusion.2) | copy-start | bytes 1540 | tf_op jit(solution)/shard_map/while
  133.5 4.3 %copy-start.7 = (f32[64,8,9,128]{3,1,2,0:T(8,128)}, f32[64,8,9,128]{3,1,2,0:T(8,128)S(1)}, u32[]{:S(2)}) copy-start(f32[64,8,9,128]{3,1,2,0:T(8,128)S(1)} %get-tuple-element.647) | copy-start | bytes 7077892 | tf_op jit(solution)/shard_map/while
  137.8 4.0 copy-start.9
  146.5 5.5 %copy-start.15 = (bf16[4096,128]{0,1:T(8,128)(2,1)}, bf16[4096,128]{0,1:T(8,128)(2,1)S(1)}, u32[]{:S(2)}) copy-start(bf16[4096,128]{0,1:T(8,128)(2,1)S(1)} %fusion.479) | copy-start | bytes 3145732 | tf_op jit(solution)/shard_map/while
  147.9 4.1 copy-start.41
  148.6 3.3 copy-start.21
  152.8 4.4 %copy-start.23 = (f32[4096]{0:T(1024)}, f32[4096]{0:T(1024)S(1)}, u32[]{:S(2)}) copy-start(f32[4096]{0:T(1024)S(1)} %fusion.481) | copy-start | bytes 49156 | tf_op jit(solution)/shard_map/while
  161.1 3.0 copy-start.6
  178.9 4.9 %copy-start.69 = (f32[128]{0:T(128)S(1)}, f32[128]{0:T(128)}, u32[]{:S(2)}) copy-start(f32[128]{0:T(128)} %get-tuple-element.687) | copy-start | bytes 1540 | tf_op jit(solution)/shard_map/while
  196.7 5.1 %copy-start.33 = (bf16[2,1152,128]{2,1,0:T(8,128)(2,1)S(1)}, bf16[2,1152,128]{2,1,0:T(8,128)(2,1)}, u32[]{:S(2)}) copy-start(bf16[2,1152,128]{2,1,0:T(8,128)(2,1)} %get-tuple-element.720) | copy-start | bytes 1769476 | tf_op jit(solution)/shard_map/while
  196.7 5.1 %copy-start.35 = (bf16[2,1152,128]{2,1,0:T(8,128)(2,1)S(1)}, bf16[2,1152,128]{2,1,0:T(8,128)(2,1)}, u32[]{:S(2)}) copy-start(bf16[2,1152,128]{2,1,0:T(8,128)(2,1)} %get-tuple-element.721) | copy-start | bytes 1769476 | tf_op jit(solution)/shard_map/while
  196.7 5.2 %copy-start.64 = (f32[2]{0:T(128)S(1)}, f32[2]{0:T(128)}, u32[]{:S(2)}) copy-start(f32[2]{0:T(128)} %get-tuple-element.723) | copy-start | bytes 28 | tf_op jit(solution)/shard_map/while
  196.7 6.5 %copy-start.27 = (bf16[128,128]{1,0:T(8,128)(2,1)S(1)}, bf16[128,128]{1,0:T(8,128)(2,1)}, u32[]{:S(2)}) copy-start(bf16[128,128]{1,0:T(8,128)(2,1)} %get-tuple-element.805) | copy-start | bytes 98308 | tf_op jit(solution)/shard_map/while
  196.8 6.5 %copy-start.31 = (pred[8,9]{0,1:T(8,128)(4,1)S(1)}, pred[8,9]{0,1:T(8,128)(4,1)}, u32[]{:S(2)}) copy-start(pred[8,9]{0,1:T(8,128)(4,1)} %get-tuple-element.839) | copy-start | bytes 220 | tf_op jit(solution)/shard_map/while
  196.8 6.5 %copy-start.54 = (f32[6,128]{1,0:T(8,128)S(1)}, f32[6,128]{1,0:T(8,128)}, u32[]{:S(2)}) copy-start(f32[6,128]{1,0:T(8,128)} %get-tuple-element.884) | copy-start | bytes 9220 | tf_op jit(solution)/shard_map/while
  196.8 6.5 %copy-start.59 = (s32[2]{0:T(128)S(1)}, s32[2]{0:T(128)}, u32[]{:S(2)}) copy-start(s32[2]{0:T(128)} %get-tuple-element.934) | copy-start | bytes 28 | tf_op jit(solution)/shard_map/while
  196.8 6.5 %copy-start.61 = (s32[2]{0:T(128)S(1)}, s32[2]{0:T(128)}, u32[]{:S(2)}) copy-start(s32[2]{0:T(128)} %get-tuple-element.966) | copy-start | bytes 28 | tf_op jit(solution)/shard_map/while
  196.8 6.5 %copy-start.63 = (s32[2]{0:T(128)S(1)}, s32[2]{0:T(128)}, u32[]{:S(2)}) copy-start(s32[2]{0:T(128)} %get-tuple-element.999) | copy-start | bytes 28 | tf_op jit(solution)/shard_map/while
  214.3 147.6 %reduce-scatter.9.cloned.1.call-start = ((), (), s32[]{:S(2)}) async-start(), calls=%async_computation.4 | async-start | bytes 2228224 | tf_op jit(solution)/shard_map/reduce_scatter | solution.py:195
  227.6 130.0 %copy-start.66 = (f32[2]{0:T(128)S(1)}, f32[2]{0:T(128)}, u32[]{:S(2)}) copy-start(f32[2]{0:T(128)} %get-tuple-element.971) | copy-start | bytes 28
  315.7 6.5 %collective-permute-start.15 = (f32[36,128]{1,0:T(8,128)S(1)}, f32[36,128]{1,0:T(8,128)S(1)}, u32[]{:S(2)}, u32[]{:S(2)}) collective-permute-start(f32[36,128]{1,0:T(8,128)S(1)} %slice.91), channel_id=1, source_target_pairs={{0,8},{1,9},{2,10},{3,11},{4,12},{5,13},{6,14},{7,15},{8,16},{9,17... | collective-permute-start | bytes 55304
  317.0 15.0 %collective-permute-start.10 = (f32[48,128]{1,0:T(8,128)S(1)}, f32[48,128]{1,0:T(8,128)S(1)}, u32[]{:S(2)}, u32[]{:S(2)}) collective-permute-start(f32[48,128]{1,0:T(8,128)S(1)} %get-tuple-element.418), channel_id=1, source_target_pairs={{0,3},{1,4},{2,5},{3,6},{4,7},{5,8},{6,9},{7,10},{8,11},{9,12},{10... | collective-permute-start | bytes 73736
  318.3 18.7 %collective-permute-start.11 = (f32[48,128]{1,0:T(8,128)S(1)}, f32[48,128]{1,0:T(8,128)S(1)}, u32[]{:S(2)}, u32[]{:S(2)}) collective-permute-start(f32[48,128]{1,0:T(8,128)S(1)} %get-tuple-element.418), channel_id=1, source_target_pairs={{0,4},{1,5},{2,6},{3,7},{4,8},{5,9},{6,10},{7,11},{8,12},{9,13},{1... | collective-permute-start | bytes 73736
  319.6 20.1 %collective-permute-start.12 = (f32[48,128]{1,0:T(8,128)S(1)}, f32[48,128]{1,0:T(8,128)S(1)}, u32[]{:S(2)}, u32[]{:S(2)}) collective-permute-start(f32[48,128]{1,0:T(8,128)S(1)} %get-tuple-element.418), channel_id=1, source_target_pairs={{0,5},{1,6},{2,7},{3,8},{4,9},{5,10},{6,11},{7,12},{8,13},{9,14},{... | collective-permute-start | bytes 73736
  320.9 21.4 %collective-permute-start.13 = (f32[48,128]{1,0:T(8,128)S(1)}, f32[48,128]{1,0:T(8,128)S(1)}, u32[]{:S(2)}, u32[]{:S(2)}) collective-permute-start(f32[48,128]{1,0:T(8,128)S(1)} %get-tuple-element.418), channel_id=1, source_target_pairs={{0,6},{1,7},{2,8},{3,9},{4,10},{5,11},{6,12},{7,13},{8,14},{9,15},... | collective-permute-start | bytes 73736
  322.2 8.5 %collective-permute-start.7 = (f32[36,128]{1,0:T(8,128)S(1)}, f32[36,128]{1,0:T(8,128)S(1)}, u32[]{:S(2)}, u32[]{:S(2)}) collective-permute-start(f32[36,128]{1,0:T(8,128)S(1)} %slice.90), channel_id=1, source_target_pairs={{0,8},{1,9},{2,10},{3,11},{4,12},{5,13},{6,14},{7,15},{8,16},{9,17... | collective-permute-start | bytes 55304
  330.7 14.8 %collective-permute-start.14 = (f32[48,128]{1,0:T(8,128)S(1)}, f32[48,128]{1,0:T(8,128)S(1)}, u32[]{:S(2)}, u32[]{:S(2)}) collective-permute-start(f32[48,128]{1,0:T(8,128)S(1)} %get-tuple-element.418), channel_id=1, source_target_pairs={{0,7},{1,8},{2,9},{3,10},{4,11},{5,12},{6,13},{7,14},{8,15},{9,16}... | collective-permute-start | bytes 73736
  332.0 16.5 %collective-permute-start.8 = (f32[48,128]{1,0:T(8,128)S(1)}, f32[48,128]{1,0:T(8,128)S(1)}, u32[]{:S(2)}, u32[]{:S(2)}) collective-permute-start(f32[48,128]{1,0:T(8,128)S(1)} %get-tuple-element.418), channel_id=1, source_target_pairs={{0,1},{1,2},{2,3},{3,4},{4,5},{5,6},{6,7},{7,8},{8,9},{9,10},{10,1... | collective-permute-start | bytes 73736
  336.9 14.0 %collective-permute-start.9 = (f32[48,128]{1,0:T(8,128)S(1)}, f32[48,128]{1,0:T(8,128)S(1)}, u32[]{:S(2)}, u32[]{:S(2)}) collective-permute-start(f32[48,128]{1,0:T(8,128)S(1)} %get-tuple-element.418), channel_id=1, source_target_pairs={{0,2},{1,3},{2,4},{3,5},{4,6},{5,7},{6,8},{7,9},{8,10},{9,11},{10,... | collective-permute-start | bytes 73736
  339.7 13.2 %collective-permute-start = (f32[48,128]{1,0:T(8,128)S(1)}, f32[48,128]{1,0:T(8,128)S(1)}, u32[]{:S(2)}, u32[]{:S(2)}) collective-permute-start(f32[48,128]{1,0:T(8,128)S(1)} %get-tuple-element.417), channel_id=1, source_target_pairs={{0,1},{1,2},{2,3},{3,4},{4,5},{5,6},{6,7},{7,8},{8,9},{9,10},{10,1... | collective-permute-start | bytes 73736
  342.3 13.6 %collective-permute-start.1 = (f32[48,128]{1,0:T(8,128)S(1)}, f32[48,128]{1,0:T(8,128)S(1)}, u32[]{:S(2)}, u32[]{:S(2)}) collective-permute-start(f32[48,128]{1,0:T(8,128)S(1)} %get-tuple-element.417), channel_id=1, source_target_pairs={{0,2},{1,3},{2,4},{3,5},{4,6},{5,7},{6,8},{7,9},{8,10},{9,11},{10,... | collective-permute-start | bytes 73736
  345.5 13.9 %collective-permute-start.2 = (f32[48,128]{1,0:T(8,128)S(1)}, f32[48,128]{1,0:T(8,128)S(1)}, u32[]{:S(2)}, u32[]{:S(2)}) collective-permute-start(f32[48,128]{1,0:T(8,128)S(1)} %get-tuple-element.417), channel_id=1, source_target_pairs={{0,3},{1,4},{2,5},{3,6},{4,7},{5,8},{6,9},{7,10},{8,11},{9,12},{10... | collective-permute-start | bytes 73736
  348.5 10.9 %collective-permute-start.3 = (f32[48,128]{1,0:T(8,128)S(1)}, f32[48,128]{1,0:T(8,128)S(1)}, u32[]{:S(2)}, u32[]{:S(2)}) collective-permute-start(f32[48,128]{1,0:T(8,128)S(1)} %get-tuple-element.417), channel_id=1, source_target_pairs={{0,4},{1,5},{2,6},{3,7},{4,8},{5,9},{6,10},{7,11},{8,12},{9,13},{1... | collective-permute-start | bytes 73736
  350.9 8.5 %collective-permute-start.4 = (f32[48,128]{1,0:T(8,128)S(1)}, f32[48,128]{1,0:T(8,128)S(1)}, u32[]{:S(2)}, u32[]{:S(2)}) collective-permute-start(f32[48,128]{1,0:T(8,128)S(1)} %get-tuple-element.417), channel_id=1, source_target_pairs={{0,5},{1,6},{2,7},{3,8},{4,9},{5,10},{6,11},{7,12},{8,13},{9,14},{... | collective-permute-start | bytes 73736
  352.9 6.5 %collective-permute-start.5 = (f32[48,128]{1,0:T(8,128)S(1)}, f32[48,128]{1,0:T(8,128)S(1)}, u32[]{:S(2)}, u32[]{:S(2)}) collective-permute-start(f32[48,128]{1,0:T(8,128)S(1)} %get-tuple-element.417), channel_id=1, source_target_pairs={{0,6},{1,7},{2,8},{3,9},{4,10},{5,11},{6,12},{7,13},{8,14},{9,15},... | collective-permute-start | bytes 73736
  355.9 3.5 collective-permute-start.6
  (89 other events, 125.2 us)
Sparse Core Ops, SparseCore 0:
  9.5 13.2 all-gather.1
  214.4 13.0 reduce-scatter.6
  229.9 82.9 reduce-scatter.8
where the time goes:
time: 419 us; the launch traced here: 416 us
  blocking collectives  125 us (30%)
  matrix products  95.9 us (23%)
  local copies, waits for them, and re-layouts  48.1 us (11%)
  other arithmetic  40.4 us (10%)
  starting transfers between devices  40.3 us (10%)
  waiting for transfers between devices  30.2 us (7%)
  between operations  18.3 us (4%)
  loops' own time  17.2 us (4%)
    unnamed x1, blocking collectives  86.5 us
    conv_general_dilated x10, matrix products, convolve(): lax.conv_general_dilated(picture, kernel, (1, 1), 'SAME', dimension_numbe...  41.9 us
    unnamed x16, starting transfers between devices  40.2 us
    psum x1, blocking collectives, local(): lax.psum((square_one, square_two, square_kv), ('dp', 'mp'))  38.8 us
    while x260, local copies, waits for them, and re-layouts  17.9 us
    another operation x1, loops' own time, local(): lax.map(one_image, (clean, noise, lowres, aug_noise, timesteps, aug_level...  17.2 us
    all_gather x1, waiting for transfers between devices, local(): piece = lax.all_gather(kv_weight, 'mp', axis=0, tiled=True)  14.8 us
    reduce_scatter x1, waiting for transfers between devices, local(): lax.psum_scatter(full_grad, 'mp', scatter_dimension=0, tiled=True)  13.2 us
  transfers between devices with their start and end apart: 19, of which 3 were waited for; matrix products, arithmetic and copies ran while one was open for 22% of the time, Pallas kernels for 0%

commit v1 on v0

--- a/solution.py
+++ b/solution.py
@@ -1,8 +1,11 @@
+import functools
 import math
 
 import jax
 import jax.numpy as jnp
 from jax import lax
+from jax.experimental import pallas as pl
+from jax.experimental.pallas import tpu as pltpu
 from jax.sharding import PartitionSpec as P
 
 S = 64
@@ -115,6 +118,151 @@
     )
     error = pred - noise
     return jnp.sum(error * error)
+
+
+def exchange_kernel(
+    n,
+    mp_size,
+    counts,
+    conv_ref,
+    kv_ref,
+    loss_ref,
+    conv_out,
+    kv_out,
+    stat_out,
+    conv_in,
+    kv_in,
+    stat_in,
+    stat_ref,
+    conv_send,
+    conv_recv,
+    kv_send,
+    kv_recv,
+    stat_send,
+    stat_recv,
+):
+    half = kv_out.shape[1]
+    me = lax.axis_index("dp") * mp_size + lax.axis_index("mp")
+
+    def target(k):
+        return lax.rem(me + k + 1, n)
+
+    def place(t):
+        return (lax.div(t, mp_size), lax.rem(t, mp_size))
+
+    def kv_block(t):
+        column = pl.multiple_of(lax.rem(t, mp_size) * half, half)
+        return kv_ref.at[lax.div(t, mp_size), :, pl.ds(column, half)]
+
+    def remote(src, dst, send, recv, k, slot):
+        return pltpu.make_async_remote_copy(
+            src_ref=src,
+            dst_ref=dst.at[slot],
+            send_sem=send.at[k],
+            recv_sem=recv.at[k],
+            device_id=place(target(k)),
+            device_id_type=pl.DeviceIdType.MESH,
+        )
+
+    def kv_copy(k):
+        return remote(kv_block(target(k)), kv_in, kv_send, kv_recv, k, k)
+
+    def conv_copy(k):
+        return remote(conv_ref.at[target(k)], conv_in, conv_send, conv_recv, k, k)
+
+    def stat_copy(k, slot):
+        return remote(stat_ref, stat_in, stat_send, stat_recv, k, slot)
+
+    def over_peers(step):
+        def body(k, carry):
+            step(k)
+            return carry
+
+        lax.fori_loop(0, n - 1, body, 0)
+
+    barrier = pltpu.get_barrier_semaphore()
+    over_peers(
+        lambda k: pl.semaphore_signal(
+            barrier,
+            inc=1,
+            device_id=place(target(k)),
+            device_id_type=pl.DeviceIdType.MESH,
+        )
+    )
+    pl.semaphore_wait(barrier, n - 1)
+
+    def start(k):
+        kv_copy(k).start()
+        conv_copy(k).start()
+
+    over_peers(start)
+    own = pl.multiple_of(lax.rem(me, mp_size) * half, half)
+    kv_out[...] = kv_ref[lax.div(me, mp_size), :, pl.ds(own, half)].astype(jnp.float32)
+    conv_out[...] = conv_ref[me].astype(jnp.float32)
+
+    def gather(k):
+        kv_copy(k).wait_recv()
+        kv_out[...] += kv_in[k].astype(jnp.float32)
+        conv_copy(k).wait_recv()
+        conv_out[...] += conv_in[k].astype(jnp.float32)
+
+    over_peers(gather)
+
+    def lanes(values):
+        folded = jnp.sum(values * values, axis=0, keepdims=True)
+        total = folded[:, :128]
+        for piece in range(1, folded.shape[1] // 128):
+            total = total + folded[:, piece * 128 : (piece + 1) * 128]
+        return total
+
+    stat_ref[...] = loss_ref[...]
+    stat_ref[0:1, :] = lanes(conv_out[0])
+    stat_ref[1:2, :] = lanes(conv_out[1])
+    stat_ref[2:3, :] = lanes(kv_out[...])
+    over_peers(lambda k: stat_copy(k, me).start())
+    stat_in[me] = stat_ref[...]
+
+    def add_stat(k):
+        stat_copy(k, lax.rem(me + n - k - 1, n)).wait_recv()
+
+    over_peers(add_stat)
+    totals = jnp.sum(jnp.sum(stat_in[...], axis=0), axis=1, keepdims=True)
+    stat_out[...] = jnp.broadcast_to(totals, stat_out.shape)
+    conv_out[0] = conv_out[0] * lax.rsqrt(totals[0:1] / counts[0] + 1e-06)
+    conv_out[1] = conv_out[1] * lax.rsqrt(totals[1:2] / counts[0] + 1e-06)
+    kv_out[...] = kv_out[...] * lax.rsqrt(totals[2:3] / counts[1] + 1e-06)
+
+    def finish(k):
+        kv_copy(k).wait_send()
+        conv_copy(k).wait_send()
+        stat_copy(k, me).wait_send()
+
+    over_peers(finish)
+
+
+def exchange(conv_blocks, kv_blocks, loss, counts, mp_size):
+    n = conv_blocks.shape[0]
+    columns = kv_blocks.shape[1]
+    half = kv_blocks.shape[2] // mp_size
+    vmem = pl.BlockSpec(memory_space=pltpu.VMEM)
+    return pl.pallas_call(
+        functools.partial(exchange_kernel, n, mp_size, counts),
+        out_shape=(
+            jax.ShapeDtypeStruct(conv_blocks.shape[1:], jnp.float32),
+            jax.ShapeDtypeStruct((columns, half), jnp.float32),
+            jax.ShapeDtypeStruct(loss.shape, jnp.float32),
+        ),
+        in_specs=[vmem] * 3,
+        out_specs=(vmem,) * 3,
+        scratch_shapes=[
+            pltpu.VMEM((n - 1,) + conv_blocks.shape[1:], conv_blocks.dtype),
+            pltpu.VMEM((n - 1, columns, half), kv_blocks.dtype),
+            pltpu.VMEM((n,) + loss.shape, jnp.float32),
+            pltpu.VMEM(loss.shape, jnp.float32),
+        ]
+        + [pltpu.SemaphoreType.DMA((n - 1,))] * 6,
+        compiler_params=pltpu.CompilerParams(collective_id=0, has_side_effects=True),
+    )(conv_blocks, kv_blocks, loss)
 
 
 def local(
@@ -179,33 +327,34 @@
     )
     local_one = jnp.sum(parts_one.astype(jnp.float32), axis=0)
     local_two = jnp.sum(parts_two.astype(jnp.float32), axis=0)
-    local_loss = jnp.sum(values)
-    loss_total = lax.psum(local_loss, ("dp", "mp"))
-    grad_one, grad_two = (
-        lax.psum_scatter(local_one, ("dp", "mp"), scatter_dimension=0, tiled=True),
-        lax.psum_scatter(local_two, ("dp", "mp"), scatter_dimension=0, tiled=True),
-    )
-    full_grad = lax.dot_general(
+    dp_size = lax.axis_size("dp")
+    mp_size = lax.axis_size("mp")
+    devices = dp_size * mp_size
+    turned = lax.dot_general(
+        parts_kv.reshape(-1, width),
         text.reshape(-1, features),
-        parts_kv.reshape(-1, width),
         (((0,), (0,)), ((), ())),
         preferred_element_type=jnp.float32,
-    )
-    row_share = lax.psum_scatter(full_grad, "mp", scatter_dimension=0, tiled=True)
-    grad_kv = lax.psum_scatter(row_share, "dp", scatter_dimension=1, tiled=True)
-    square_one = jnp.sum(grad_one * grad_one)
-    square_two = jnp.sum(grad_two * grad_two)
-    square_kv = jnp.sum(grad_kv * grad_kv)
-    total_one, total_two, total_kv = lax.psum((square_one, square_two, square_kv), ("dp", "mp"))
-    conv_count = conv_one.shape[0] * conv_one.shape[1]
-    kv_count = half * lax.axis_size("mp") * width
-    conv_one_update = grad_one * lax.rsqrt(total_one / conv_count + 1e-06)
-    conv_two_update = grad_two * lax.rsqrt(total_two / conv_count + 1e-06)
-    kv_update = grad_kv * lax.rsqrt(total_kv / kv_count + 1e-06)
-    loss_mean = loss_total / (
-        images * lax.axis_size(("dp", "mp")) * clean.shape[1] * clean.shape[2]
-    )
-    return (conv_one_update, conv_two_update, kv_update, loss_mean)
+    ).astype(jnp.bfloat16)
+    rows = conv_one.shape[0] // devices
+    conv_blocks = jnp.stack(
+        [
+            local_one.reshape(devices, rows, conv_one.shape[1]),
+            local_two.reshape(devices, rows, conv_one.shape[1]),
+        ],
+        axis=1,
+    ).astype(jnp.bfloat16)
+    loss = jnp.zeros((8, 128), jnp.float32).at[3, 0].set(jnp.sum(values))
+    counts = (conv_one.shape[0] * conv_one.shape[1], half * mp_size * width)
+    conv_updates, kv_turned, stats = exchange(
+        conv_blocks,
+        turned.reshape(dp_size, width // dp_size, features),
+        loss,
+        counts,
+        mp_size,
+    )
+    loss_mean = stats[3, 0] / (images * devices * clean.shape[1] * clean.shape[2])
+    return (conv_updates[0], conv_updates[1], kv_turned.T, loss_mean)
 
 
 def solution(mesh):

time: 419 us -> 316 us (0.75)
  blocking collectives: 125 us -> 0 us
  Pallas kernels: 0 us -> 82.8 us
  starting transfers between devices: 40.3 us -> 0.04 us
  waiting for transfers between devices: 30.2 us -> 15.5 us
  local copies, waits for them, and re-layouts: 48.1 us -> 52.8 us
    unnamed x1 -> x0, blocking collectives: 86.5 us -> none
    pallas_call x0 -> x1, Pallas kernels: none -> 82.8 us  [exchange(): pl.pallas_call(functools.partial(exchange_kernel, n, mp_size, counts), ou...]
    unnamed x16 -> x0, starting transfers between devices: 40.2 us -> none
    psum x1 -> x0, blocking collectives: 38.8 us -> none  [local(): lax.psum((square_one, square_two, square_kv), ('dp', 'mp'))]
    reduce_scatter x2 -> x0, waiting for transfers between devices: 13.2 us -> none  [the longest x1 13.2 us: local(): lax.psum_scatter(full_grad, 'mp', scatter_dimension=0, tiled=True)]
  transfers between devices with their start and end apart: 19 -> 1, of which waited for: 3 -> 1; matrix products, arithmetic and copies ran while one was open for 22% -> 0% of each run, Pallas kernels for 0% -> 0%
where the time goes in v1:
time: 316 us; the launch traced here: 313 us
  matrix products  96.3 us (30%)
  Pallas kernels  82.8 us (26%)
  local copies, waits for them, and re-layouts  52.8 us (17%)
  other arithmetic  36.8 us (12%)
  between operations  16.2 us (5%)
  waiting for transfers between devices  15.5 us (5%)
  loops' own time  13.1 us (4%)
    pallas_call x1, Pallas kernels, exchange(): pl.pallas_call(functools.partial(exchange_kernel, n, mp_size, counts), ou...  82.8 us
    conv_general_dilated x10, matrix products, convolve(): lax.conv_general_dilated(picture, kernel, (1, 1), 'SAME', dimension_numbe...  42 us
    while x260, local copies, waits for them, and re-layouts  19.4 us
    all_gather x1, waiting for transfers between devices, local(): piece = lax.all_gather(kv_weight, 'mp', axis=0, tiled=True)  14.8 us
    another operation x1, loops' own time, local(): lax.map(one_image, (clean, noise, lowres, aug_noise, timesteps, aug_level...  13.1 us
    dot_general x4, matrix products, image_loss(): jnp.einsum('kc,pc->kp', w_head, h_out.astype(jnp.bfloat16), preferred_ele...  12.1 us
    dynamic_slice x14, local copies, waits for them, and re-layouts, local(): lax.map(one_image, (clean, noise, lowres, aug_noise, timesteps, aug_level...  11.3 us
    dot_general x12, matrix products, image_loss(): jnp.dot(probs, keys_values[:, width + lower:width + upper], preferred_ele...  10.3 us
  transfers between devices with their start and end apart: 1, of which 1 were waited for; matrix products, arithmetic and copies ran while one was open for 0% of the time, Pallas kernels for 0%

profile of v1, /device:TPU:0, one launch (start us, length us, event | category | flops | bytes accessed | tf_op | source)
XLA Modules:
  0.0 313.5 jit_solution(10042923766533026229)
XLA Ops:
  8.0 14.8 %all-gather.2.cloned.1.call-done = bf16[4096,256]{1,0:T(8,128)(2,1)} async-done(((bf16[2048,256]{1,0:T(8,128)(2,1)}), bf16[4096,256]{1,0:T(8,128)(2,1)}) %all-gather.2.cloned.1.call-update) | async-done | bytes 2097168 | tf_op jit(solution)/shard_map/all_gather | solution.py:291
  22.9 3.0 fusion.284
  25.9 184.2 %while.20 = (s32[]{:T(128)}, bf16[2,1152,128]{2,1,0:T(8,128)(2,1)}, bf16[2,1152,128]{2,1,0:T(8,128)(2,1)}, bf16[2,128,256]{1,2,0:T(8,128)(2,1)}, f32[2]{0:T(128)...) while((s32[]{:T(128)}, bf16[2,1152,128]{2,1,0:T(8,128)(2,1)}, ...), condition=%wide.region_22.23_spmd, body=%wide.region_0.22_spmd.sunk | while | flops 8245876736 | bytes 325935616 | solution.py:325
  27.7 0.9 constant_dynamic-slice_fusion.8
  28.7 0.9 constant_dynamic-slice_fusion.11
  31.1 0.9 constant_dynamic-slice_fusion.10
  32.1 0.9 constant_dynamic-slice_fusion.9
  33.1 3.5 %fusion.462 = (f32[128]{0:T(128)S(1)}, f32[4096,128]{1,0:T(8,128)S(1)}) fusion(f32[6,128]{1,0:T(8,128)S(1)} %get-tuple-element.747, f32[3,4096]{1,0:T(4,128)S(1)} %fusion.460, f32[3,4096]{1,0:T(4,128)S(1)} %fusion.461), kind=kOutput, calls=%fused_computation.376.clone.1 | convolution fusion | flops 38297472 | bytes 2199040 | tf_op jit(solution)/shard_map/while/body/eval_jaxpr/kp,kc->pc/dot_general | solution.py:37
  40.1 3.0 select_reduce_fusion.8
  44.1 0.8 fusion.471
  46.0 1.2 fusion.472
  48.1 3.1 fusion.474
  51.9 1.2 copy.113
  58.0 2.1 convert_reduce_fusion.5
  60.1 1.4 convolution_convert_fusion.20
  62.4 2.1 convert_reduce_fusion.4
  64.5 1.0 copy-done.13
  65.6 1.5 convolution_convert_fusion.19
  67.1 4.3 %multiply_reduce_fusion.14 = (f32[]{:T(128)}, f32[3,4096]{1,0:T(4,128)}) fusion(f32[1,3,4096]{2,0,1:T(1,128)S(1)} %constant_dynamic-slice_fusion.8, bf16[3,128]{1,0:T(4,128)(2,1)} %get-tuple-element.755, f32[4096,128]{1,0:T(8,128)} %copy-done.1, bf16[128,128]{1,0:T(8,128)(2,1)} %get-tuple-element.754, ...), kind=kOutput, calls=%fused_computation.201.clone.1 | convolution fusion | flops 140546048 | bytes 3277572 | tf_op jit(solution)/shard_map/while/body/eval_jaxpr/jvp(kc,pc->kp)/dot_general | solution.py:116
  71.4 1.7 convolution_convert_fusion.21
  73.1 1.2 convolution_convert_fusion.22
  82.1 1.1 copy-done.2
  83.2 1.5 multiply_reduce_fusion.17
  89.2 5.1 %select_reduce_fusion.10 = (f32[128]{0:T(128)S(1)}, f32[64,8,9,128]{3,1,2,0:T(8,128)S(1)}) fusion(f32[64,8,9,128]{3,1,2,0:T(8,128)S(1)} %copy-done.8, f32[128]{0:T(128)S(1)} %copy-done.40, pred[8,9]{0,1:T(8,128)(4,1)} %get-tuple-element.830, f32[128]{0:T(128)S(1)} %copy-done.49, f32[128]{0:T(128)S(1)} %copy-done.47, f32[128]{0:T(128)S(1)} %copy-done.51, ...), kind=kOutput, calls=%fused_computation.51.clone.1 | convolution fusion | flops 1360920448 | bytes 6425160 | tf_op jit(solution)/shard_map/while/body/eval_jaxpr/transpose(jvp())/conv_general_dilated | solution.py:67
  94.6 1.4 select_reduce_fusion.11
  99.3 5.0 %fusion.497 = bf16[3,3,128,128,1]{3,2,1,4,0:T(8,128)(2,1)S(1)} fusion(bf16[64,8,9,128,1]{3,1,4,2,0:T(8,128)(2,1)S(1)} %fusion.493, bf16[64,8,9,128,1]{3,1,4,2,0:T(8,128)(2,1)S(1)} %copy.117, bf16[64,8,9,128,1]{3,1,4,2,0:T(8,128)(2,1)S(1)} %fusion.494, f32[128]{0:T(128)S(1)} %fusion.496, pred[8,9]{0,1:T(8,128)(4,1)} %get-tuple-element.830, ...), kind=kOutput, calls=%fused_computation.101.clone.1 | convolution fusion | flops 1360281600 | bytes 8554568 | tf_op jit(solution)/shard_map/while/body/eval_jaxpr/transpose(jvp())/conv_general_dilated | solution.py:67
  104.4 1.8 fusion.489
  107.4 4.8 %fusion.490 = bf16[3,3,128,128,1]{3,2,1,4,0:T(8,128)(2,1)S(1)} fusion(bf16[64,8,9,128,1]{3,0,2,1,4:T(8,128)(2,1)S(1)} %bitcast.341, bf16[64,8,9,128,1]{3,1,2,0,4:T(8,128)(2,1)S(1)} %maximum_bitcast_fusion.8, bf16[64,8,9,128,1]{3,1,2,0,4:T(8,128)(2,1)S(1)} %fusion.489, bf16[64,8,9,128,1]{3,1,2,0,4:T(8,128)(2,1)S(1)} %maximum_bitcast_fusion.9), kind=kOutput, calls=%fused_computation.100.clone.1 | convolution fusion | flops 1348337664 | bytes 5013504 | tf_op jit(solution)/shard_map/while/body/eval_jaxpr/transpose(jvp())/conv_general_dilated | solution.py:67
  112.3 0.8 copy-done.36
  118.5 0.9 constant_dynamic-slice_fusion.8
  119.4 0.9 constant_dynamic-slice_fusion.11
  121.8 0.9 constant_dynamic-slice_fusion.10
  122.8 0.9 constant_dynamic-slice_fusion.9
  123.8 3.5 %fusion.462 = (f32[128]{0:T(128)S(1)}, f32[4096,128]{1,0:T(8,128)S(1)}) fusion(f32[6,128]{1,0:T(8,128)S(1)} %get-tuple-element.747, f32[3,4096]{1,0:T(4,128)S(1)} %fusion.460, f32[3,4096]{1,0:T(4,128)S(1)} %fusion.461), kind=kOutput, calls=%fused_computation.376.clone.1 | convolution fusion | flops 38297472 | bytes 2199040 | tf_op jit(solution)/shard_map/while/body/eval_jaxpr/kp,kc->pc/dot_general | solution.py:37
  130.9 3.0 select_reduce_fusion.8
  134.9 0.8 fusion.471
  136.8 1.4 fusion.472
  139.1 3.1 fusion.474
  142.9 1.2 copy.113
  149.0 2.1 convert_reduce_fusion.5
  151.1 1.4 convolution_convert_fusion.20
  153.4 2.1 convert_reduce_fusion.4
  155.5 1.0 copy-done.13
  156.6 1.5 convolution_convert_fusion.19
  158.0 4.3 %multiply_reduce_fusion.14 = (f32[]{:T(128)}, f32[3,4096]{1,0:T(4,128)}) fusion(f32[1,3,4096]{2,0,1:T(1,128)S(1)} %constant_dynamic-slice_fusion.8, bf16[3,128]{1,0:T(4,128)(2,1)} %get-tuple-element.755, f32[4096,128]{1,0:T(8,128)} %copy-done.1, bf16[128,128]{1,0:T(8,128)(2,1)} %get-tuple-element.754, ...), kind=kOutput, calls=%fused_computation.201.clone.1 | convolution fusion | flops 140546048 | bytes 3277572 | tf_op jit(solution)/shard_map/while/body/eval_jaxpr/jvp(kc,pc->kp)/dot_general | solution.py:116
  162.4 1.7 convolution_convert_fusion.21
  164.1 1.2 convolution_convert_fusion.22
  173.0 1.1 copy-done.2
  174.1 1.5 multiply_reduce_fusion.17
  180.1 4.9 %select_reduce_fusion.10 = (f32[128]{0:T(128)S(1)}, f32[64,8,9,128]{3,1,2,0:T(8,128)S(1)}) fusion(f32[64,8,9,128]{3,1,2,0:T(8,128)S(1)} %copy-done.8, f32[128]{0:T(128)S(1)} %copy-done.40, pred[8,9]{0,1:T(8,128)(4,1)} %get-tuple-element.830, f32[128]{0:T(128)S(1)} %copy-done.49, f32[128]{0:T(128)S(1)} %copy-done.47, f32[128]{0:T(128)S(1)} %copy-done.51, ...), kind=kOutput, calls=%fused_computation.51.clone.1 | convolution fusion | flops 1360920448 | bytes 6425160 | tf_op jit(solution)/shard_map/while/body/eval_jaxpr/transpose(jvp())/conv_general_dilated | solution.py:67
  185.3 1.4 select_reduce_fusion.11
  190.0 5.0 %fusion.497 = bf16[3,3,128,128,1]{3,2,1,4,0:T(8,128)(2,1)S(1)} fusion(bf16[64,8,9,128,1]{3,1,4,2,0:T(8,128)(2,1)S(1)} %fusion.493, bf16[64,8,9,128,1]{3,1,4,2,0:T(8,128)(2,1)S(1)} %copy.117, bf16[64,8,9,128,1]{3,1,4,2,0:T(8,128)(2,1)S(1)} %fusion.494, f32[128]{0:T(128)S(1)} %fusion.496, pred[8,9]{0,1:T(8,128)(4,1)} %get-tuple-element.830, ...), kind=kOutput, calls=%fused_computation.101.clone.1 | convolution fusion | flops 1360281600 | bytes 8554568 | tf_op jit(solution)/shard_map/while/body/eval_jaxpr/transpose(jvp())/conv_general_dilated | solution.py:67
  195.1 1.8 fusion.489
  198.1 5.0 %fusion.490 = bf16[3,3,128,128,1]{3,2,1,4,0:T(8,128)(2,1)S(1)} fusion(bf16[64,8,9,128,1]{3,0,2,1,4:T(8,128)(2,1)S(1)} %bitcast.341, bf16[64,8,9,128,1]{3,1,2,0,4:T(8,128)(2,1)S(1)} %maximum_bitcast_fusion.8, bf16[64,8,9,128,1]{3,1,2,0,4:T(8,128)(2,1)S(1)} %fusion.489, bf16[64,8,9,128,1]{3,1,2,0,4:T(8,128)(2,1)S(1)} %maximum_bitcast_fusion.9), kind=kOutput, calls=%fused_computation.100.clone.1 | convolution fusion | flops 1348337664 | bytes 5013504 | tf_op jit(solution)/shard_map/while/body/eval_jaxpr/transpose(jvp())/conv_general_dilated | solution.py:67
  203.2 0.8 copy-done.36
  210.1 1.3 reduce.6
  211.5 1.3 reduce.7
  212.9 2.1 fusion.281
  215.6 1.2 scatter.4.loss_ref
  216.8 0.9 pad_maximum_fusion.2.conv_ref
  217.7 82.8 %shard_map.183 = (f32[2,36,128]{2,1,0:T(8,128)}, f32[16,2048]{1,0:T(8,128)}, f32[8,128]{1,0:T(8,128)}) custom-call(bf16[32,2,36,128]{3,2,1,0:T(8,128)(2,1)} %pad_maximum_fusion.2.conv_ref, bf16[16,16,4096]{2,1,0:T(8,128)(2,1)} %bitcast.342, f32[8,128]{1,0:T(8,128)} %scatter.4.loss_ref), custom_call_target="tpu_custom_call" | custom-call | tf_op jit(solution)/shard_map/pallas_call | solution.py:248
  300.5 1.4 slice_bitcast_fusion.1
  301.8 1.2 slice.87
  303.7 1.6 copy.149
  (435 shorter events, 65.5 us)
Async XLA Ops:
  7.2 15.7 %copy-start = (bf16[2,128,4096]{2,1,0:T(8,128)(2,1)S(1)}, bf16[2,128,4096]{2,1,0:T(8,128)(2,1)}, u32[]{:S(2)}) copy-start(bf16[2,128,4096]{2,1,0:T(8,128)(2,1)} %param.27) | copy-start | bytes 6291460
  7.2 15.7 %all-gather.2.cloned.1.call-start = ((), (), s32[]{:S(2)}) async-start(), calls=%async_computation | async-start | bytes 3145728 | tf_op jit(solution)/shard_map/all_gather | solution.py:291
  8.0 17.9 %copy-start.26 = (bf16[128,128]{1,0:T(8,128)(2,1)S(1)}, bf16[128,128]{1,0:T(8,128)(2,1)}, u32[]{:S(2)}) copy-start(bf16[128,128]{1,0:T(8,128)(2,1)} %param.33) | copy-start | bytes 98308
  8.0 17.9 %copy-start.30 = (pred[8,9]{0,1:T(8,128)(4,1)S(1)}, pred[8,9]{0,1:T(8,128)(4,1)}, u32[]{:S(2)}) copy-start(pred[8,9]{0,1:T(8,128)(4,1)} %constant.596) | copy-start | bytes 220
  8.0 17.8 %copy-start.54 = (f32[6,128]{1,0:T(8,128)S(1)}, f32[6,128]{1,0:T(8,128)}, u32[]{:S(2)}) copy-start(f32[6,128]{1,0:T(8,128)} %param.28) | copy-start | bytes 9220
  8.0 17.8 %copy-start.59 = (s32[2]{0:T(128)S(1)}, s32[2]{0:T(128)}, u32[]{:S(2)}) copy-start(s32[2]{0:T(128)} %param.24) | copy-start | bytes 28
  8.0 17.8 %copy-start.61 = (s32[2]{0:T(128)S(1)}, s32[2]{0:T(128)}, u32[]{:S(2)}) copy-start(s32[2]{0:T(128)} %param.25) | copy-start | bytes 28
  8.0 17.8 %copy-start.63 = (s32[2]{0:T(128)S(1)}, s32[2]{0:T(128)}, u32[]{:S(2)}) copy-start(s32[2]{0:T(128)} %param.26) | copy-start | bytes 28
  36.6 17.9 %copy-start.68 = (s32[128]{0:T(128)}, s32[128]{0:T(128)S(1)}, u32[]{:S(2)}) copy-start(s32[128]{0:T(128)S(1)} %and_select_fusion.2) | copy-start | bytes 1540 | tf_op jit(solution)/shard_map/while
  43.2 4.0 %copy-start.7 = (f32[64,8,9,128]{3,1,2,0:T(8,128)}, f32[64,8,9,128]{3,1,2,0:T(8,128)S(1)}, u32[]{:S(2)}) copy-start(f32[64,8,9,128]{3,1,2,0:T(8,128)S(1)} %get-tuple-element.637) | copy-start | bytes 7077892 | tf_op jit(solution)/shard_map/while
  43.2 2.0 copy-start.25
  43.4 2.1 copy-start.39
  46.0 2.1 copy-start.57
  47.2 4.0 %copy-start.9 = (bf16[64,1,8,9,128]{4,2,3,0,1:T(8,128)(2,1)}, bf16[64,1,8,9,128]{4,2,3,0,1:T(8,128)(2,1)S(1)}, u32[]{:S(2)}) copy-start(bf16[64,1,8,9,128]{4,2,3,0,1:T(8,128)(2,1)S(1)} %fusion.472) | copy-start | bytes 3538948 | tf_op jit(solution)/shard_map/while
  53.7 2.1 copy-start.1
  53.9 1.9 copy-start.37
  55.8 5.7 %copy-start.15 = (bf16[4096,128]{0,1:T(8,128)(2,1)}, bf16[4096,128]{0,1:T(8,128)(2,1)S(1)}, u32[]{:S(2)}) copy-start(bf16[4096,128]{0,1:T(8,128)(2,1)S(1)} %fusion.477) | copy-start | bytes 3145732 | tf_op jit(solution)/shard_map/while
  57.2 4.3 %copy-start.41 = (pred[128]{0:T(512)(128)(4,1)}, pred[128]{0:T(512)(128)(4,1)S(1)}, u32[]{:S(2)}) copy-start(pred[128]{0:T(512)(128)(4,1)S(1)} %iota_compare_fusion.6) | copy-start | bytes 388 | tf_op jit(solution)/shard_map/while
  57.6 2.5 copy-start.3
  58.0 3.6 %copy-start.21 = (f32[4096]{0:T(1024)}, f32[4096]{0:T(1024)S(1)}, u32[]{:S(2)}) copy-start(f32[4096]{0:T(1024)S(1)} %fusion.481) | copy-start | bytes 49156 | tf_op jit(solution)/shard_map/while
  60.1 1.9 copy-start.11
  62.1 2.5 copy-start.5
  62.4 4.7 %copy-start.23 = (f32[4096]{0:T(1024)}, f32[4096]{0:T(1024)S(1)}, u32[]{:S(2)}) copy-start(f32[4096]{0:T(1024)S(1)} %fusion.479) | copy-start | bytes 49156 | tf_op jit(solution)/shard_map/while
  71.4 2.9 copy-start.24
  71.4 3.0 copy-start.6
  89.2 5.1 %copy-start.70 = (f32[128]{0:T(128)S(1)}, f32[128]{0:T(128)}, u32[]{:S(2)}) copy-start(f32[128]{0:T(128)} %get-tuple-element.677) | copy-start | bytes 1540 | tf_op jit(solution)/shard_map/while
  107.3 4.9 %copy-start.33 = (bf16[2,1152,128]{2,1,0:T(8,128)(2,1)S(1)}, bf16[2,1152,128]{2,1,0:T(8,128)(2,1)}, u32[]{:S(2)}) copy-start(bf16[2,1152,128]{2,1,0:T(8,128)(2,1)} %get-tuple-element.710) | copy-start | bytes 1769476 | tf_op jit(solution)/shard_map/while
  107.3 4.9 %copy-start.35 = (bf16[2,1152,128]{2,1,0:T(8,128)(2,1)S(1)}, bf16[2,1152,128]{2,1,0:T(8,128)(2,1)}, u32[]{:S(2)}) copy-start(bf16[2,1152,128]{2,1,0:T(8,128)(2,1)} %get-tuple-element.711) | copy-start | bytes 1769476 | tf_op jit(solution)/shard_map/while
  107.3 5.8 %copy-start.65 = (f32[2]{0:T(128)S(1)}, f32[2]{0:T(128)}, u32[]{:S(2)}) copy-start(f32[2]{0:T(128)} %get-tuple-element.713) | copy-start | bytes 28 | tf_op jit(solution)/shard_map/while
  107.3 7.1 %copy-start.27 = (bf16[128,128]{1,0:T(8,128)(2,1)S(1)}, bf16[128,128]{1,0:T(8,128)(2,1)}, u32[]{:S(2)}) copy-start(bf16[128,128]{1,0:T(8,128)(2,1)} %get-tuple-element.799) | copy-start | bytes 98308 | tf_op jit(solution)/shard_map/while
  107.3 7.1 %copy-start.31 = (pred[8,9]{0,1:T(8,128)(4,1)S(1)}, pred[8,9]{0,1:T(8,128)(4,1)}, u32[]{:S(2)}) copy-start(pred[8,9]{0,1:T(8,128)(4,1)} %get-tuple-element.830) | copy-start | bytes 220 | tf_op jit(solution)/shard_map/while
  107.3 7.1 %copy-start.55 = (f32[6,128]{1,0:T(8,128)S(1)}, f32[6,128]{1,0:T(8,128)}, u32[]{:S(2)}) copy-start(f32[6,128]{1,0:T(8,128)} %get-tuple-element.860) | copy-start | bytes 9220 | tf_op jit(solution)/shard_map/while
  107.3 7.1 %copy-start.60 = (s32[2]{0:T(128)S(1)}, s32[2]{0:T(128)}, u32[]{:S(2)}) copy-start(s32[2]{0:T(128)} %get-tuple-element.892) | copy-start | bytes 28 | tf_op jit(solution)/shard_map/while
  107.4 7.1 %copy-start.62 = (s32[2]{0:T(128)S(1)}, s32[2]{0:T(128)}, u32[]{:S(2)}) copy-start(s32[2]{0:T(128)} %get-tuple-element.924) | copy-start | bytes 28 | tf_op jit(solution)/shard_map/while
  107.4 7.1 %copy-start.64 = (s32[2]{0:T(128)S(1)}, s32[2]{0:T(128)}, u32[]{:S(2)}) copy-start(s32[2]{0:T(128)} %get-tuple-element.957) | copy-start | bytes 28 | tf_op jit(solution)/shard_map/while
  127.3 18.2 %copy-start.68 = (s32[128]{0:T(128)}, s32[128]{0:T(128)S(1)}, u32[]{:S(2)}) copy-start(s32[128]{0:T(128)S(1)} %and_select_fusion.2) | copy-start | bytes 1540 | tf_op jit(solution)/shard_map/while
  133.9 4.3 %copy-start.7 = (f32[64,8,9,128]{3,1,2,0:T(8,128)}, f32[64,8,9,128]{3,1,2,0:T(8,128)S(1)}, u32[]{:S(2)}) copy-start(f32[64,8,9,128]{3,1,2,0:T(8,128)S(1)} %get-tuple-element.637) | copy-start | bytes 7077892 | tf_op jit(solution)/shard_map/while
  133.9 2.0 copy-start.25
  134.1 2.1 copy-start.39
  136.8 2.3 copy-start.57
  138.2 4.0 %copy-start.9 = (bf16[64,1,8,9,128]{4,2,3,0,1:T(8,128)(2,1)}, bf16[64,1,8,9,128]{4,2,3,0,1:T(8,128)(2,1)S(1)}, u32[]{:S(2)}) copy-start(bf16[64,1,8,9,128]{4,2,3,0,1:T(8,128)(2,1)S(1)} %fusion.472) | copy-start | bytes 3538948 | tf_op jit(solution)/shard_map/while
  144.7 2.1 copy-start.1
  144.9 1.9 copy-start.37
  146.8 5.7 %copy-start.15 = (bf16[4096,128]{0,1:T(8,128)(2,1)}, bf16[4096,128]{0,1:T(8,128)(2,1)S(1)}, u32[]{:S(2)}) copy-start(bf16[4096,128]{0,1:T(8,128)(2,1)S(1)} %fusion.477) | copy-start | bytes 3145732 | tf_op jit(solution)/shard_map/while
  148.2 4.3 %copy-start.41 = (pred[128]{0:T(512)(128)(4,1)}, pred[128]{0:T(512)(128)(4,1)S(1)}, u32[]{:S(2)}) copy-start(pred[128]{0:T(512)(128)(4,1)S(1)} %iota_compare_fusion.6) | copy-start | bytes 388 | tf_op jit(solution)/shard_map/while
  148.6 2.5 copy-start.3
  148.9 3.6 %copy-start.21 = (f32[4096]{0:T(1024)}, f32[4096]{0:T(1024)S(1)}, u32[]{:S(2)}) copy-start(f32[4096]{0:T(1024)S(1)} %fusion.481) | copy-start | bytes 49156 | tf_op jit(solution)/shard_map/while
  151.1 1.9 copy-start.11
  153.0 2.5 copy-start.5
  153.4 4.7 %copy-start.23 = (f32[4096]{0:T(1024)}, f32[4096]{0:T(1024)S(1)}, u32[]{:S(2)}) copy-start(f32[4096]{0:T(1024)S(1)} %fusion.479) | copy-start | bytes 49156 | tf_op jit(solution)/shard_map/while
  162.4 2.9 copy-start.24
  162.4 2.9 copy-start.6
  180.1 4.9 %copy-start.70 = (f32[128]{0:T(128)S(1)}, f32[128]{0:T(128)}, u32[]{:S(2)}) copy-start(f32[128]{0:T(128)} %get-tuple-element.677) | copy-start | bytes 1540 | tf_op jit(solution)/shard_map/while
  198.0 5.1 %copy-start.33 = (bf16[2,1152,128]{2,1,0:T(8,128)(2,1)S(1)}, bf16[2,1152,128]{2,1,0:T(8,128)(2,1)}, u32[]{:S(2)}) copy-start(bf16[2,1152,128]{2,1,0:T(8,128)(2,1)} %get-tuple-element.710) | copy-start | bytes 1769476 | tf_op jit(solution)/shard_map/while
  198.0 5.1 %copy-start.35 = (bf16[2,1152,128]{2,1,0:T(8,128)(2,1)S(1)}, bf16[2,1152,128]{2,1,0:T(8,128)(2,1)}, u32[]{:S(2)}) copy-start(bf16[2,1152,128]{2,1,0:T(8,128)(2,1)} %get-tuple-element.711) | copy-start | bytes 1769476 | tf_op jit(solution)/shard_map/while
  198.0 6.1 %copy-start.65 = (f32[2]{0:T(128)S(1)}, f32[2]{0:T(128)}, u32[]{:S(2)}) copy-start(f32[2]{0:T(128)} %get-tuple-element.713) | copy-start | bytes 28 | tf_op jit(solution)/shard_map/while
  198.0 7.4 %copy-start.27 = (bf16[128,128]{1,0:T(8,128)(2,1)S(1)}, bf16[128,128]{1,0:T(8,128)(2,1)}, u32[]{:S(2)}) copy-start(bf16[128,128]{1,0:T(8,128)(2,1)} %get-tuple-element.799) | copy-start | bytes 98308 | tf_op jit(solution)/shard_map/while
  198.0 7.4 %copy-start.31 = (pred[8,9]{0,1:T(8,128)(4,1)S(1)}, pred[8,9]{0,1:T(8,128)(4,1)}, u32[]{:S(2)}) copy-start(pred[8,9]{0,1:T(8,128)(4,1)} %get-tuple-element.830) | copy-start | bytes 220 | tf_op jit(solution)/shard_map/while
  198.0 7.4 %copy-start.55 = (f32[6,128]{1,0:T(8,128)S(1)}, f32[6,128]{1,0:T(8,128)}, u32[]{:S(2)}) copy-start(f32[6,128]{1,0:T(8,128)} %get-tuple-element.860) | copy-start | bytes 9220 | tf_op jit(solution)/shard_map/while
  198.1 7.3 %copy-start.60 = (s32[2]{0:T(128)S(1)}, s32[2]{0:T(128)}, u32[]{:S(2)}) copy-start(s32[2]{0:T(128)} %get-tuple-element.892) | copy-start | bytes 28 | tf_op jit(solution)/shard_map/while
  198.1 7.3 %copy-start.62 = (s32[2]{0:T(128)S(1)}, s32[2]{0:T(128)}, u32[]{:S(2)}) copy-start(s32[2]{0:T(128)} %get-tuple-element.924) | copy-start | bytes 28 | tf_op jit(solution)/shard_map/while
  198.1 7.3 %copy-start.64 = (s32[2]{0:T(128)S(1)}, s32[2]{0:T(128)}, u32[]{:S(2)}) copy-start(s32[2]{0:T(128)} %get-tuple-element.957) | copy-start | bytes 28 | tf_op jit(solution)/shard_map/while
  210.1 2.8 copy-start.45
  212.9 2.1 copy-start.67
  (72 other events, 87.6 us)
Sparse Core Ops, SparseCore 0:
  9.5 13.2 all-gather.1
